TPU v7x, 32 devices: a whole 2x2x4 slice. The times are simulated.
32 devices in a mesh: group: 4 (over x, core), replica: 8 (over z, y).
Axes of the slice: x: 2, y: 2, z: 4, core: 2. Of those that a mesh axis runs over, the one named last changes fastest.
Arguments:
- activations: float32 [16, 1024, 768], P('replica', 'group'), may hold values from -6 to 6
- out_grad: float32 [16, 1024, 768], P('replica', 'group'), may hold values from -6 to 6
- picture_ids: int32 [16, 1024], P('replica'), may hold values from -1 to 9, as said below
- ln1_gain: float32 [768], P('group'), may hold values from 0.5 to 1.5
- ln1_bias: float32 [768], P('group'), may hold values from -3 to 3
- w_query: float32 [768, 768], P(None, 'group'), may hold values from -0.3125 to 0.3125
- q_bias: float32 [768], P('group'), may hold values from -3 to 3
- w_key: float32 [768, 768], P(None, 'group'), may hold values from -0.3125 to 0.3125
- w_value: float32 [768, 768], P(None, 'group'), may hold values from -0.21875 to 0.21875
- v_bias: float32 [768], P('group'), may hold values from -3 to 3
- w_out: float32 [768, 768], P('group'), may hold values from -1.75 to 1.75
- out_bias: float32 [768], P('group'), may hold values from -3 to 3
- ln2_gain: float32 [768], P('group'), may hold values from 0.5 to 1.5
- ln2_bias: float32 [768], P('group'), may hold values from -3 to 3
- w_fc1: float32 [768, 3072], P(None, 'group'), may hold values from -0.21875 to 0.21875
- fc1_bias: float32 [3072], P('group'), may hold values from -3 to 3
- w_fc2: float32 [3072, 768], P('group'), may hold values from -0.109375 to 0.109375
- fc2_bias: float32 [768], P('group'), may hold values from -3 to 3
Outputs:
- output: float32 [16, 1024, 768], P('replica', 'group')
- grad_input: float32 [16, 1024, 768], P('replica', 'group')
- grad_ln1_gain: float32 [768], P('group')
- grad_ln1_bias: float32 [768], P('group')
- grad_w_query: float32 [768, 768], P(None, 'group')
- grad_q_bias: float32 [768], P('group')
- grad_w_key: float32 [768, 768], P(None, 'group')
- grad_w_value: float32 [768, 768], P(None, 'group')
- grad_v_bias: float32 [768], P('group')
- grad_w_out: float32 [768, 768], P('group')
- grad_out_bias: float32 [768], P('group')
- grad_ln2_gain: float32 [768], P('group')
- grad_ln2_bias: float32 [768], P('group')
- grad_w_fc1: float32 [768, 3072], P(None, 'group')
- grad_fc1_bias: float32 [3072], P('group')
- grad_w_fc2: float32 [3072, 768], P('group')
- grad_fc2_bias: float32 [768], P('group')
Inputs may be any that keep to these rules, and one draw needn't show every extreme that they name: `picture_ids`: each row holds whole pictures numbered 0, 1, 2 and so on from its start, each of 100 to 1024 patches, followed by padding marked -1.
All inputs are finite; a program needn't handle non-finite values.
Results may differ from a plain program's by a relative error of at most 0.04.
Values may be sent and summed in bfloat16 or wider, within the bound.
No kernel may reach another device: no remote copies, remote signals or barrier semaphores. Data moves between devices by JAX's collectives and lax.ppermute only.
A program may use at most 256 MiB of HBM per device.

v0:
```python
import jax
import jax.numpy as jnp
from jax import lax
from jax.sharding import PartitionSpec as P

HEADS = 12
HEAD_DIM = 64
EPS = 1e-06
MASKED = -1e30


def to_float(values):
    return values.astype(jnp.float32)


def normalize(values):
    centred = values - jnp.mean(values, axis=-1, keepdims=True)
    inverse = lax.rsqrt(jnp.mean(centred * centred, axis=-1, keepdims=True) + EPS)
    return (centred * inverse, inverse)


def norm_back(grad_hat, normed_hat, inverse):
    return inverse * (
        grad_hat
        - jnp.mean(grad_hat, axis=-1, keepdims=True)
        - normed_hat * jnp.mean(grad_hat * normed_hat, axis=-1, keepdims=True)
    )


def gelu_tanh(values):
    return jax.nn.gelu(values, approximate=True)


def heads_of(values):
    return values.reshape(values.shape[0], HEADS, HEAD_DIM)


def scores_of(query_rows, key_rows, query_ids, key_ids):
    raw_scores = jnp.einsum(
        "qhe,khe->hqk", heads_of(query_rows), heads_of(key_rows), preferred_element_type=jnp.float32
    ) * HEAD_DIM ** (-0.5)
    allowed = query_ids[:, None] == key_ids[None, :]
    return jnp.where(allowed[None], raw_scores, MASKED)


def attend_row(pieces):
    query_rows, key_rows, value_rows, query_ids, key_ids = pieces
    scores = scores_of(query_rows, key_rows, query_ids, key_ids)
    row_top = jnp.max(scores, axis=-1, keepdims=True)
    exponent = jnp.exp(scores - row_top)
    row_total = jnp.sum(exponent, axis=-1, keepdims=True)
    probability = (exponent / row_total).astype(jnp.bfloat16)
    attended = jnp.einsum(
        "hqk,khe->qhe", probability, heads_of(value_rows), preferred_element_type=jnp.float32
    )
    return (
        attended.reshape(query_rows.shape[0], -1).astype(jnp.bfloat16),
        (row_top + jnp.log(row_total))[..., 0],
    )


def attend_back(pieces):
    query_rows, key_rows, value_rows, query_ids, key_ids, logsum, grad_rows = pieces
    scores = scores_of(query_rows, key_rows, query_ids, key_ids)
    probability = jnp.exp(scores - logsum[..., None])
    grad_heads = heads_of(grad_rows)
    grad_value = jnp.einsum(
        "hqk,qhe->khe",
        probability.astype(jnp.bfloat16),
        grad_heads,
        preferred_element_type=jnp.float32,
    )
    grad_probs = jnp.einsum(
        "qhe,khe->hqk", grad_heads, heads_of(value_rows), preferred_element_type=jnp.float32
    )
    centre = jnp.sum(probability * grad_probs, axis=-1, keepdims=True)
    grad_scores = (probability * (grad_probs - centre)).astype(jnp.bfloat16)
    score_scale = HEAD_DIM ** (-0.5)
    grad_query = (
        jnp.einsum(
            "hqk,khe->qhe", grad_scores, heads_of(key_rows), preferred_element_type=jnp.float32
        )
        * score_scale
    )
    grad_key = (
        jnp.einsum(
            "hqk,qhe->khe", grad_scores, heads_of(query_rows), preferred_element_type=jnp.float32
        )
        * score_scale
    )
    query_count = query_rows.shape[0]
    key_count = key_rows.shape[0]
    return (
        grad_query.reshape(query_count, -1).astype(jnp.bfloat16),
        grad_key.reshape(key_count, -1),
        grad_value.reshape(key_count, -1),
    )


def per_device(
    activations,
    out_grad,
    picture_ids,
    ln1_gain,
    ln1_bias,
    w_query,
    q_bias,
    w_key,
    w_value,
    v_bias,
    w_out,
    out_bias,
    ln2_gain,
    ln2_bias,
    w_fc1,
    fc1_bias,
    w_fc2,
    fc2_bias,
):
    row_block, local_len, width = activations.shape
    row_total = row_block * local_len
    offset = lax.axis_index("group") * local_len
    own_ids = lax.dynamic_slice_in_dim(picture_ids, offset, local_len, 1)
    (
        query_full,
        key_full,
        value_full,
        out_full,
        gain_one,
        shift_one,
        bias_query,
        bias_value,
        bias_out,
        gain_two,
        shift_two,
        bias_fc2,
    ) = (
        lax.all_gather(w_query.astype(jnp.bfloat16), "group", axis=1, tiled=True),
        lax.all_gather(w_key.astype(jnp.bfloat16), "group", axis=1, tiled=True),
        lax.all_gather(w_value.astype(jnp.bfloat16), "group", axis=1, tiled=True),
        lax.all_gather(w_out.astype(jnp.bfloat16), "group", axis=0, tiled=True),
        lax.all_gather(ln1_gain.astype(jnp.bfloat16), "group", axis=0, tiled=True),
        lax.all_gather(ln1_bias.astype(jnp.bfloat16), "group", axis=0, tiled=True),
        lax.all_gather(q_bias.astype(jnp.bfloat16), "group", axis=0, tiled=True),
        lax.all_gather(v_bias.astype(jnp.bfloat16), "group", axis=0, tiled=True),
        lax.all_gather(out_bias.astype(jnp.bfloat16), "group", axis=0, tiled=True),
        lax.all_gather(ln2_gain.astype(jnp.bfloat16), "group", axis=0, tiled=True),
        lax.all_gather(ln2_bias.astype(jnp.bfloat16), "group", axis=0, tiled=True),
        lax.all_gather(fc2_bias.astype(jnp.bfloat16), "group", axis=0, tiled=True),
    )
    inputs = activations.reshape(row_total, width)
    hat_one, inverse_one = normalize(inputs)
    normed_one = (hat_one * to_float(gain_one) + to_float(shift_one)).astype(jnp.bfloat16)
    queries = (
        jnp.dot(normed_one, query_full, preferred_element_type=jnp.float32) + to_float(bias_query)
    ).astype(jnp.bfloat16)
    keys_new = jnp.dot(normed_one, key_full, preferred_element_type=jnp.float32).astype(
        jnp.bfloat16
    )
    values_new = (
        jnp.dot(normed_one, value_full, preferred_element_type=jnp.float32) + to_float(bias_value)
    ).astype(jnp.bfloat16)
    key_all, value_all = (
        lax.all_gather(keys_new.reshape(row_block, local_len, width), "group", axis=1, tiled=True),
        lax.all_gather(
            values_new.reshape(row_block, local_len, width), "group", axis=1, tiled=True
        ),
    )
    query_rows = queries.reshape(row_block, local_len, width)
    attended, logsum = lax.map(attend_row, (query_rows, key_all, value_all, own_ids, picture_ids))
    attended = attended.reshape(row_total, width)
    middle = inputs + (
        jnp.dot(attended, out_full, preferred_element_type=jnp.float32) + to_float(bias_out)
    )
    hat_two, inverse_two = normalize(middle)
    normed_two = (hat_two * to_float(gain_two) + to_float(shift_two)).astype(jnp.bfloat16)
    fc1_full, fc2_full, bias_fc1 = (
        lax.all_gather(w_fc1.astype(jnp.bfloat16), "group", axis=1, tiled=True),
        lax.all_gather(w_fc2.astype(jnp.bfloat16), "group", axis=0, tiled=True),
        lax.all_gather(fc1_bias.astype(jnp.bfloat16), "group", axis=0, tiled=True),
    )
    hidden = jnp.dot(normed_two, fc1_full, preferred_element_type=jnp.float32) + to_float(bias_fc1)
    gelu_value, gelu_pull = jax.vjp(gelu_tanh, hidden)
    activated = gelu_value.astype(jnp.bfloat16)
    mlp_output = jnp.dot(activated, fc2_full, preferred_element_type=jnp.float32)
    output = middle + (mlp_output + to_float(bias_fc2))
    valid_rows = (own_ids >= 0).astype(jnp.float32).reshape(row_total, 1)
    grad_out = out_grad.reshape(row_total, width) * valid_rows
    grad_mlp = grad_out.astype(jnp.bfloat16)
    grad_bias_fc2 = jnp.sum(to_float(grad_mlp), axis=0)
    grad_activated = jnp.dot(grad_mlp, fc2_full.T, preferred_element_type=jnp.float32)
    grad_fc2 = jnp.dot(activated.T, grad_mlp, preferred_element_type=jnp.float32)
    grad_hidden = gelu_pull(grad_activated)[0].astype(jnp.bfloat16)
    grad_fc1 = jnp.dot(normed_two.T, grad_hidden, preferred_element_type=jnp.float32)
    grad_bias_fc1 = jnp.sum(to_float(grad_hidden), axis=0)
    grad_normed_two = jnp.dot(grad_hidden, fc1_full.T, preferred_element_type=jnp.float32)
    grad_fc1, grad_fc2, grad_bias_fc1 = (
        lax.psum_scatter(
            grad_fc1.astype(jnp.bfloat16), "group", scatter_dimension=1, tiled=True
        ).astype(jnp.float32),
        lax.psum_scatter(
            grad_fc2.astype(jnp.bfloat16), "group", scatter_dimension=0, tiled=True
        ).astype(jnp.float32),
        lax.psum_scatter(
            grad_bias_fc1.astype(jnp.bfloat16), "group", scatter_dimension=0, tiled=True
        ).astype(jnp.float32),
    )
    grad_gain_two = jnp.sum(grad_normed_two * hat_two, axis=0)
    grad_shift_two = jnp.sum(grad_normed_two, axis=0)
    grad_middle = grad_out + norm_back(grad_normed_two * to_float(gain_two), hat_two, inverse_two)
    grad_branch = grad_middle.astype(jnp.bfloat16)
    grad_bias_out = jnp.sum(to_float(grad_branch), axis=0)
    grad_out_full = jnp.dot(attended.T, grad_branch, preferred_element_type=jnp.float32)
    grad_attended = jnp.dot(grad_branch, out_full.T, preferred_element_type=jnp.float32).astype(
        jnp.bfloat16
    )
    grad_att_rows = grad_attended.reshape(row_block, local_len, width)
    grad_queries, key_parts, value_parts = lax.map(
        attend_back, (query_rows, key_all, value_all, own_ids, picture_ids, logsum, grad_att_rows)
    )
    grad_keys, grad_values = (
        lax.psum_scatter(
            key_parts.astype(jnp.bfloat16), "group", scatter_dimension=1, tiled=True
        ).astype(jnp.float32),
        lax.psum_scatter(
            value_parts.astype(jnp.bfloat16), "group", scatter_dimension=1, tiled=True
        ).astype(jnp.float32),
    )
    grad_queries = grad_queries.reshape(row_total, width)
    grad_keys = grad_keys.reshape(row_total, width).astype(jnp.bfloat16)
    grad_values = grad_values.reshape(row_total, width).astype(jnp.bfloat16)
    grad_query_full = jnp.dot(normed_one.T, grad_queries, preferred_element_type=jnp.float32)
    grad_key_full = jnp.dot(normed_one.T, grad_keys, preferred_element_type=jnp.float32)
    grad_value_full = jnp.dot(normed_one.T, grad_values, preferred_element_type=jnp.float32)
    grad_bias_query = jnp.sum(to_float(grad_queries), axis=0)
    grad_bias_value = jnp.sum(to_float(grad_values), axis=0)
    grad_normed_one = jnp.dot(grad_queries, query_full.T, preferred_element_type=jnp.float32)
    grad_normed_one = grad_normed_one + jnp.dot(
        grad_keys, key_full.T, preferred_element_type=jnp.float32
    )
    grad_normed_one = grad_normed_one + jnp.dot(
        grad_values, value_full.T, preferred_element_type=jnp.float32
    )
    grad_gain_one = jnp.sum(grad_normed_one * hat_one, axis=0)
    grad_shift_one = jnp.sum(grad_normed_one, axis=0)
    grad_input = grad_middle + norm_back(grad_normed_one * to_float(gain_one), hat_one, inverse_one)
    (
        grad_query_full,
        grad_key_full,
        grad_value_full,
        grad_out_full,
        grad_gain_one,
        grad_shift_one,
        grad_bias_query,
        grad_bias_value,
        grad_bias_out,
        grad_gain_two,
        grad_shift_two,
        grad_bias_fc2,
    ) = (
        lax.psum_scatter(
            grad_query_full.astype(jnp.bfloat16), "group", scatter_dimension=1, tiled=True
        ).astype(jnp.float32),
        lax.psum_scatter(
            grad_key_full.astype(jnp.bfloat16), "group", scatter_dimension=1, tiled=True
        ).astype(jnp.float32),
        lax.psum_scatter(
            grad_value_full.astype(jnp.bfloat16), "group", scatter_dimension=1, tiled=True
        ).astype(jnp.float32),
        lax.psum_scatter(
            grad_out_full.astype(jnp.bfloat16), "group", scatter_dimension=0, tiled=True
        ).astype(jnp.float32),
        lax.psum_scatter(
            grad_gain_one.astype(jnp.bfloat16), "group", scatter_dimension=0, tiled=True
        ).astype(jnp.float32),
        lax.psum_scatter(
            grad_shift_one.astype(jnp.bfloat16), "group", scatter_dimension=0, tiled=True
        ).astype(jnp.float32),
        lax.psum_scatter(
            grad_bias_query.astype(jnp.bfloat16), "group", scatter_dimension=0, tiled=True
        ).astype(jnp.float32),
        lax.psum_scatter(
            grad_bias_value.astype(jnp.bfloat16), "group", scatter_dimension=0, tiled=True
        ).astype(jnp.float32),
        lax.psum_scatter(
            grad_bias_out.astype(jnp.bfloat16), "group", scatter_dimension=0, tiled=True
        ).astype(jnp.float32),
        lax.psum_scatter(
            grad_gain_two.astype(jnp.bfloat16), "group", scatter_dimension=0, tiled=True
        ).astype(jnp.float32),
        lax.psum_scatter(
            grad_shift_two.astype(jnp.bfloat16), "group", scatter_dimension=0, tiled=True
        ).astype(jnp.float32),
        lax.psum_scatter(
            grad_bias_fc2.astype(jnp.bfloat16), "group", scatter_dimension=0, tiled=True
        ).astype(jnp.float32),
    )
    (
        grad_query_full,
        grad_key_full,
        grad_value_full,
        grad_out_full,
        grad_gain_one,
        grad_shift_one,
        grad_bias_query,
        grad_bias_value,
        grad_bias_out,
        grad_gain_two,
        grad_shift_two,
        grad_bias_fc2,
        grad_fc1,
        grad_fc2,
        grad_bias_fc1,
    ) = lax.psum(
        (
            grad_query_full,
            grad_key_full,
            grad_value_full,
            grad_out_full,
            grad_gain_one,
            grad_shift_one,
            grad_bias_query,
            grad_bias_value,
            grad_bias_out,
            grad_gain_two,
            grad_shift_two,
            grad_bias_fc2,
            grad_fc1,
            grad_fc2,
            grad_bias_fc1,
        ),
        "replica",
    )
    return (
        output.reshape(row_block, local_len, width),
        grad_input.reshape(row_block, local_len, width),
        grad_gain_one,
        grad_shift_one,
        grad_query_full,
        grad_bias_query,
        grad_key_full,
        grad_value_full,
        grad_bias_value,
        grad_out_full,
        grad_bias_out,
        grad_gain_two,
        grad_shift_two,
        grad_fc1,
        grad_bias_fc1,
        grad_fc2,
        grad_bias_fc2,
    )


def solution(mesh):
    placed = (
        P("replica", "group", None),
        P("replica", "group", None),
        P("replica", None),
        P("group"),
        P("group"),
        P(None, "group"),
        P("group"),
        P(None, "group"),
        P(None, "group"),
        P("group"),
        P("group", None),
        P("group"),
        P("group"),
        P("group"),
        P(None, "group"),
        P("group"),
        P("group", None),
        P("group"),
    )
    return jax.shard_map(
        per_device,
        mesh=mesh,
        in_specs=placed,
        out_specs=(
            P("replica", "group", None),
            P("replica", "group", None),
            P("group"),
            P("group"),
            P(None, "group"),
            P("group"),
            P(None, "group"),
            P(None, "group"),
            P("group"),
            P("group", None),
            P("group"),
            P("group"),
            P("group"),
            P(None, "group"),
            P("group"),
            P("group", None),
            P("group"),
        ),
        check_vma=False,
    )
```

profile of v0, /device:TPU:0, one launch (start us, length us, event | category | flops | bytes accessed | tf_op | source)
XLA Modules:
  0.0 935.0 jit_solution(2342156140588591705)
XLA Ops:
  7.3 1.9 convert_element_type.265
  13.8 13.2 %all-reduce.19 = (bf16[768]{0:T(1024)(128)(2,1)S(1)}, bf16[768]{0:T(1024)(128)(2,1)S(1)}, bf16[768]{0:T(1024)(128)(2,1)S(1)}, bf16[768]{0:T(1024)(128)(2,1)S(1)}...) all-reduce(bf16[768]{0:T(1024)(128)(2,1)S(1)} %dynamic-update-slice, ...), channel_id=1, replica_groups=mesh['group'=4,'replica'=8] {'group'}, use_global_device_ids=true, to_apply=%add.1 | all-reduce | flops 5376 | bytes 21504
  28.7 1.9 all-gather.10.cloned.1.call-done
  30.6 2.1 add_convert_fusion.3
  33.9 16.3 %all-gather.16.cloned.1.call-done = bf16[768,768]{0,1:T(8,128)(2,1)} async-done(((bf16[768,192]{0,1:T(8,128)(2,1)}), bf16[768,768]{0,1:T(8,128)(2,1)}) %all-gather.16.cloned.1.call-update) | async-done | bytes 1179664 | tf_op jit(solution)/shard_map/all_gather | solution.py:139
  50.2 2.1 convolution_convert_fusion.4
  54.4 2.8 convert_element_type.283
  57.3 3.0 convert_element_type.287
  62.3 5.2 all-gather
  69.9 2.3 add_convert_fusion.2
  72.5 28.4 %all-gather.12.cloned.1.call-done = bf16[2,1024,768]{1,2,0:T(8,128)(2,1)} async-done(((bf16[2,256,768]{1,2,0:T(8,128)(2,1)}), bf16[2,1024,768]{1,2,0:T(8,128)(2,1)}) %all-gather.12.cloned.1.call-update) | async-done | bytes 3145744 | tf_op jit(solution)/shard_map/all_gather | solution.py:165
  100.9 30.4 %all-gather.18.cloned.1.call-done = bf16[2,1024,768]{1,2,0:T(8,128)(2,1)} async-done(((bf16[2,256,768]{1,2,0:T(8,128)(2,1)}), bf16[2,1024,768]{1,2,0:T(8,128)(2,1)}) %all-gather.18.cloned.1.call-update) | async-done | bytes 3145744 | tf_op jit(solution)/shard_map/all_gather | solution.py:164
  131.2 29.5 %while.26 = (s32[]{:T(128)}, bf16[2,256,768]{2,1,0:T(8,128)(2,1)}, f32[2,12,256]{2,1,0:T(8,128)}, bf16[2,1024,768]{1,2,0:T(8,128)(2,1)}, s32[2,256]{1,0:T(2,128)...) while((s32[]{:T(128)}, bf16[2,256,768]{2,1,0:T(8,128)(2,1)}, ...), condition=%wide.region_5.6_spmd, body=%wide.region_2.5_spmd.sunk | while | flops 843510784 | bytes 51499116 | solution.py:170
  132.3 2.2 constant_dynamic-slice_fusion.23
  134.6 2.3 fusion.100
  136.9 3.6 fusion.101
  141.1 3.9 fusion.102
  147.0 2.2 constant_dynamic-slice_fusion.23
  149.2 2.3 fusion.100
  151.5 3.6 fusion.101
  155.8 3.9 fusion.102
  160.7 2.6 fusion.32
  164.8 25.6 %all-gather.22.cloned.1.call-done = bf16[768,3072]{1,0:T(8,128)(2,1)} async-done(((bf16[768,768]{1,0:T(8,128)(2,1)}), bf16[768,3072]{1,0:T(8,128)(2,1)}) %all-gather.22.cloned.1.call-update) | async-done | bytes 4718608 | tf_op jit(solution)/shard_map/all_gather | solution.py:178
  190.4 8.2 fusion.28
  198.6 31.4 %all-gather.24.cloned.1.call-done = bf16[3072,768]{1,0:T(8,128)(2,1)} async-done(((bf16[768,768]{1,0:T(8,128)(2,1)}), bf16[3072,768]{1,0:T(8,128)(2,1)}) %all-gather.24.cloned.1.call-update) | async-done | bytes 4718608 | tf_op jit(solution)/shard_map/all_gather | solution.py:179
  230.0 9.8 %fusion.29 = (bf16[3072]{0:T(1024)(128)(2,1)}, bf16[512,3072]{1,0:T(8,128)(2,1)S(1)}) fusion(f32[512,3072]{1,0:T(8,128)} %fusion.28, f32[3072]{0:T(1024)S(1)} %bitcast.212, bf16[512,768]{1,0:T(8,128)(2,1)S(1)} %copy-done.22, bf16[3072,768]{1,0:T(8,128)(2,1)} %all-gather.24.cloned.1.call-done), kind=kOutput, calls=%fused_computation.108 | convolution fusion | flops 2450519040 | bytes 14960640 | tf_op jit(solution)/shard_map/dot_general | solution.py:191
  239.8 3.5 multiply_reduce_fusion.1
  245.7 109.7 %while.27 = (s32[]{:T(128)}, bf16[2,256,768]{1,2,0:T(8,128)(2,1)}, bf16[2,1024,768]{2,1,0:T(8,128)(2,1)}, bf16[2,1024,768]{2,1,0:T(8,128)(2,1)}, bf16[2,1024,768...) while((s32[]{:T(128)}, bf16[2,256,768]{1,2,0:T(8,128)(2,1)}, ...), condition=%wide.region_12.13_spmd, body=%wide.region_10.12_spmd.sunk | while | flops 2062676992 | bytes 238015056 | solution.py:218
  246.1 2.1 constant_dynamic-slice_fusion.27
  248.3 6.4 fusion.113
  258.3 11.5 %multiply_reduce_fusion.10 = (f32[12,256]{1,0:T(8,128)S(1)}, f32[12,256,1024]{2,1,0:T(8,128)}) fusion(f32[12,256,1024]{2,1,0:T(8,128)} %fusion.113, f32[12,256]{1,0:T(8,128)S(1)} %dynamic-slice_bitcast_fusion.2, pred[256,1024]{1,0:T(8,128)(4,1)S(1)} %broadcast_compare_fusion.5, bf16[256,12,64]{0,2,1:T(8,128)(2,1)S(1)} %bitcast.188, ...), kind=kOutput, calls=%fused_computation.18.clone.1 | convolution fusion | flops 418378752 | bytes 27418624 | tf_op jit(solution)/shard_map/while/body/eval_jaxpr/qhe,khe->hqk/dot_general | solution.py:73
  270.9 6.7 multiply_convert_fusion.6
  281.8 9.0 fusion.115
  290.8 2.7 copy.97
  293.5 3.5 constant_dynamic-update-slice_fusion.9
  297.9 2.0 fusion.114
  300.8 2.1 constant_dynamic-slice_fusion.27
  302.9 6.4 fusion.113
  313.0 11.5 %multiply_reduce_fusion.10 = (f32[12,256]{1,0:T(8,128)S(1)}, f32[12,256,1024]{2,1,0:T(8,128)}) fusion(f32[12,256,1024]{2,1,0:T(8,128)} %fusion.113, f32[12,256]{1,0:T(8,128)S(1)} %dynamic-slice_bitcast_fusion.2, pred[256,1024]{1,0:T(8,128)(4,1)S(1)} %broadcast_compare_fusion.5, bf16[256,12,64]{0,2,1:T(8,128)(2,1)S(1)} %bitcast.188, ...), kind=kOutput, calls=%fused_computation.18.clone.1 | convolution fusion | flops 418378752 | bytes 27418624 | tf_op jit(solution)/shard_map/while/body/eval_jaxpr/qhe,khe->hqk/dot_general | solution.py:73
  325.6 6.7 multiply_convert_fusion.6
  336.5 9.0 fusion.115
  345.5 2.7 copy.97
  348.2 3.4 constant_dynamic-update-slice_fusion.9
  352.6 2.0 fusion.114
  358.3 3.0 bitcast_convert_fusion.2
  361.4 2.9 convolution_convert_fusion.2
  364.4 29.1 %reduce-scatter.9.cloned.1.call-done = bf16[2,256,768]{2,1,0:T(8,128)(2,1)} async-done(((bf16[2,1024,768]{2,1,0:T(8,128)(2,1)}), bf16[2,256,768]{2,1,0:T(8,128)(2,1)}) %reduce-scatter.9.cloned.1.call-update) | async-done | bytes 786448 | tf_op jit(solution)/shard_map/reduce_scatter | solution.py:222
  393.6 3.2 bitcast_convert_fusion.1
  396.9 37.2 %reduce-scatter.11.cloned.1.call-done = bf16[2,256,768]{2,1,0:T(8,128)(2,1)} async-done(((bf16[2,1024,768]{2,1,0:T(8,128)(2,1)}), bf16[2,256,768]{2,1,0:T(8,128)(2,1)}) %reduce-scatter.11.cloned.1.call-update) | async-done | bytes 786448 | tf_op jit(solution)/shard_map/reduce_scatter | solution.py:225
  434.1 3.3 bitcast_convert_fusion
  437.5 7.4 convolution_convert_fusion.1
  445.6 8.9 convolution_convert_fusion
  458.3 2.3 copy.57
  461.9 3.4 fusion.34
  465.4 26.0 %reduce-scatter.19.cloned.1.call-done = bf16[192,768]{1,0:T(8,128)(2,1)} async-done(((bf16[768,768]{1,0:T(8,128)(2,1)}), bf16[192,768]{1,0:T(8,128)(2,1)}) %reduce-scatter.19.cloned.1.call-update) | async-done | bytes 294928 | tf_op jit(solution)/shard_map/reduce_scatter | solution.py:270
  492.7 2.4 fusion.35
  495.3 2.4 multiply_reduce_fusion.2
  497.7 10.3 %all-reduce.18 = (bf16[768]{0:T(1024)(128)(2,1)S(1)}, bf16[768]{0:T(1024)(128)(2,1)S(1)}, bf16[768]{0:T(1024)(128)(2,1)S(1)}, bf16[768]{0:T(1024)(128)(2,1)S(1)}...) all-reduce(bf16[768]{0:T(1024)(128)(2,1)S(1)} %dynamic-update-slice, ...), channel_id=1, replica_groups=mesh['group'=4,'replica'=8] {'group'}, use_global_device_ids=true, to_apply=%add.7 | all-reduce | flops 9984 | bytes 39936
  508.6 3.2 multiply_add_fusion
  511.8 9.3 add_add_fusion.1
  521.1 27.5 %reduce-scatter.17.cloned.1.call-done = bf16[768,192]{0,1:T(8,128)(2,1)} async-done(((bf16[768,768]{0,1:T(8,128)(2,1)}), bf16[768,192]{0,1:T(8,128)(2,1)}) %reduce-scatter.17.cloned.1.call-update) | async-done | bytes 294928 | tf_op jit(solution)/shard_map/reduce_scatter | solution.py:267
  548.6 50.2 %reduce-scatter.21.cloned.1.call-done = bf16[768,768]{1,0:T(8,128)(2,1)} async-done(((bf16[768,3072]{1,0:T(8,128)(2,1)}), bf16[768,768]{1,0:T(8,128)(2,1)}) %reduce-scatter.21.cloned.1.call-update) | async-done | bytes 1179664 | tf_op jit(solution)/shard_map/reduce_scatter | solution.py:198
  598.8 50.5 %reduce-scatter.23.cloned.1.call-done = bf16[768,768]{1,0:T(8,128)(2,1)} async-done(((bf16[3072,768]{1,0:T(8,128)(2,1)}), bf16[768,768]{1,0:T(8,128)(2,1)}) %reduce-scatter.23.cloned.1.call-update) | async-done | bytes 1179664 | tf_op jit(solution)/shard_map/reduce_scatter | solution.py:201
  649.3 279.1 %all-reduce.21 = (f32[192]{0:T(256)}, f32[192]{0:T(256)}, f32[768,192]{0,1:T(8,128)}, f32[192]{0:T(256)}, f32[768,192]{0,1:T(8,128)}, /*index=5*/f32[768,192]{0,...) all-reduce(f32[192]{0:T(256)S(1)} %dynamic-slice_convert_fusion.8, ...), channel_id=1, replica_groups=mesh['group'=4,'replica'=8] {'replica'}, use_global_device_ids=true, to_apply=%region_19.20 | all-reduce | flops 1771776 | bytes 10635264 | tf_op jit(solution)/shard_map/psum | solution.py:314
  (335 shorter events, 53.1 us)
Async XLA Ops:
  7.2 2.9 copy-start.26
  7.2 3.7 copy-start.64
  7.2 3.8 copy-start.65
  7.2 3.8 copy-start.66
  7.2 3.8 copy-start.67
  7.3 3.8 copy-start.68
  7.3 3.8 copy-start.69
  7.3 3.8 copy-start.70
  7.3 23.3 %all-gather.10.cloned.1.call-start = ((), (), s32[]{:S(2)}) async-start(), calls=%async_computation.8 | async-start | bytes 1474560 | tf_op jit(solution)/shard_map/all_gather | solution.py:140
  9.2 17.8 %copy-start.5 = (f32[2,256,768]{2,1,0:T(8,128)S(1)}, f32[2,256,768]{2,1,0:T(8,128)}, u32[]{:S(2)}) copy-start(f32[2,256,768]{2,1,0:T(8,128)} %param.22) | copy-start | bytes 4718596
  9.2 41.0 %all-gather.16.cloned.1.call-start = ((), (), s32[]{:S(2)}) async-start(), calls=%async_computation.11 | async-start | bytes 1474560 | tf_op jit(solution)/shard_map/all_gather | solution.py:139
  10.1 59.8 %all-gather.14.cloned.1.call-start = ((), (), s32[]{:S(2)}) async-start(), calls=%async_computation.10 | async-start | bytes 1474560 | tf_op jit(solution)/shard_map/all_gather | solution.py:138
  10.9 90.0 %all-gather.12.cloned.1.call-start = ((), (), s32[]{:S(2)}) async-start(), calls=%async_computation.9 | async-start | bytes 3932160 | tf_op jit(solution)/shard_map/all_gather | solution.py:165
  28.7 21.5 %copy-start.23 = (bf16[512,768]{1,0:T(8,128)(2,1)}, bf16[512,768]{1,0:T(8,128)(2,1)S(1)}, u32[]{:S(2)}) copy-start(bf16[512,768]{1,0:T(8,128)(2,1)S(1)} %add_convert_fusion.4) | copy-start | bytes 2359300
  33.8 97.4 %all-gather.18.cloned.1.call-start = ((), (), s32[]{:S(2)}) async-start(), calls=%async_computation.12 | async-start | bytes 3932160 | tf_op jit(solution)/shard_map/all_gather | solution.py:164
  53.5 107.2 %all-gather.20.cloned.1.call-start = ((), (), s32[]{:S(2)}) async-start(), calls=%async_computation.13 | async-start | bytes 1474560 | tf_op jit(solution)/shard_map/all_gather | solution.py:141
  54.3 136.0 %all-gather.22.cloned.1.call-start = ((), (), s32[]{:S(2)}) async-start(), calls=%async_computation.14 | async-start | bytes 5898240 | tf_op jit(solution)/shard_map/all_gather | solution.py:178
  57.2 5.1 copy-start.56
  57.2 10.9 %copy-start.12 = (f32[2,256,768]{2,1,0:T(8,128)S(1)}, f32[2,256,768]{2,1,0:T(8,128)}, u32[]{:S(2)}) copy-start(f32[2,256,768]{2,1,0:T(8,128)} %param.23) | copy-start | bytes 4718596
  57.2 172.7 %all-gather.24.cloned.1.call-start = ((), (), s32[]{:S(2)}) async-start(), calls=%async_computation.15 | async-start | bytes 5898240 | tf_op jit(solution)/shard_map/all_gather | solution.py:179
  60.3 333.3 %reduce-scatter.9.cloned.1.call-start = ((), (), s32[]{:S(2)}) async-start(), calls=%async_computation.16 | async-start | bytes 3932160 | tf_op jit(solution)/shard_map/reduce_scatter | solution.py:222
  61.0 182.3 %copy-start.46 = (f32[768]{0:T(1024)}, f32[768]{0:T(1024)S(1)}, u32[]{:S(2)}) copy-start(f32[768]{0:T(1024)S(1)} %convert_element_type.279) | copy-start | bytes 9220
  61.0 129.4 %copy-start.57 = (f32[768]{0:T(1024)}, f32[768]{0:T(1024)S(1)}, u32[]{:S(2)}) copy-start(f32[768]{0:T(1024)S(1)} %convert_element_type.281) | copy-start | bytes 9220
  62.3 6.9 copy-start.44
  163.3 80.0 %copy-start.42 = (f32[512]{0:T(512)}, f32[512]{0:T(512)S(1)}, u32[]{:S(2)}) copy-start(f32[512]{0:T(512)S(1)} %broadcast_multiply_fusion.4) | copy-start | bytes 6148
  164.8 78.5 %copy-start.53 = (f32[512]{0:T(512)}, f32[512]{0:T(512)S(1)}, u32[]{:S(2)}) copy-start(f32[512]{0:T(512)S(1)} %add_rsqrt_fusion) | copy-start | bytes 6148
  164.8 65.2 %copy-start.22 = (bf16[512,768]{1,0:T(8,128)(2,1)S(1)}, bf16[512,768]{1,0:T(8,128)(2,1)}, u32[]{:S(2)}) copy-start(bf16[512,768]{1,0:T(8,128)(2,1)} %fusion.21) | copy-start | bytes 2359300
  164.8 65.2 %copy-start.48 = (f32[4,1,768]{2,1,0:T(1,128)S(1)}, f32[4,1,768]{2,1,0:T(1,128)}, u32[]{:S(2)}) copy-start(f32[4,1,768]{2,1,0:T(1,128)} %convert_element_type.326) | copy-start | bytes 36868
  230.0 9.8 %copy-start.15 = (f32[512,768]{1,0:T(8,128)S(1)}, f32[512,768]{1,0:T(8,128)}, u32[]{:S(2)}) copy-start(f32[512,768]{1,0:T(8,128)} %copy-done.14) | copy-start | bytes 4718596
  230.0 9.8 %copy-start.62 = (bf16[768,3072]{1,0:T(8,128)(2,1)S(1)}, bf16[768,3072]{1,0:T(8,128)(2,1)}, u32[]{:S(2)}) copy-start(bf16[768,3072]{1,0:T(8,128)(2,1)} %all-gather.22.cloned.1.call-done) | copy-start | bytes 14155780
  239.7 3.6 copy-start.72
  239.7 3.6 copy-start.13
  239.7 3.6 copy-start.45
  246.1 9.3 copy-start.32
  246.1 10.3 %copy-start.17 = (bf16[2,256,768]{2,1,0:T(8,128)(2,1)}, bf16[2,256,768]{2,1,0:T(8,128)(2,1)S(1)}, u32[]{:S(2)}) copy-start(bf16[2,256,768]{2,1,0:T(8,128)(2,1)S(1)} %get-tuple-element.477) | copy-start | bytes 2359300 | tf_op jit(solution)/shard_map/while
  255.6 14.3 %copy-start.3 = (pred[256,1024]{1,0:T(8,128)(4,1)}, pred[256,1024]{1,0:T(8,128)(4,1)S(1)}, u32[]{:S(2)}) copy-start(pred[256,1024]{1,0:T(8,128)(4,1)S(1)} %broadcast_compare_fusion.5) | copy-start | bytes 786436 | tf_op jit(solution)/shard_map/while
  258.3 11.6 %slice-start = ((s8[12582912]{0:T(1024)(128)(4,1)}), s8[4194304]{0:T(1024)(128)(4,1)S(1)}, s32[]{:S(2)}) async-start(s8[12582912]{0:T(1024)(128)(4,1)} %bitcast.175), calls=%async_computation.24 | async-start | bytes 8388608 | tf_op jit(solution)/shard_map/while
  258.3 11.6 %slice-start.1 = ((s8[12582912]{0:T(1024)(128)(4,1)}), s8[4194304]{0:T(1024)(128)(4,1)S(1)}, s32[]{:S(2)}) async-start(s8[12582912]{0:T(1024)(128)(4,1)} %bitcast.175), calls=%async_computation.25 | async-start | bytes 8388608 | tf_op jit(solution)/shard_map/while
  258.3 12.6 %slice-start.2 = ((s8[12582912]{0:T(1024)(128)(4,1)}), s8[4194304]{0:T(1024)(128)(4,1)S(1)}, s32[]{:S(2)}) async-start(s8[12582912]{0:T(1024)(128)(4,1)} %bitcast.175), calls=%async_computation.26 | async-start | bytes 8388608 | tf_op jit(solution)/shard_map/while
  293.5 4.4 copy-start.1
  297.9 2.8 copy-start.18
  297.9 2.8 copy-start.33
  300.8 9.3 copy-start.32
  300.8 10.3 %copy-start.17 = (bf16[2,256,768]{2,1,0:T(8,128)(2,1)}, bf16[2,256,768]{2,1,0:T(8,128)(2,1)S(1)}, u32[]{:S(2)}) copy-start(bf16[2,256,768]{2,1,0:T(8,128)(2,1)S(1)} %get-tuple-element.477) | copy-start | bytes 2359300 | tf_op jit(solution)/shard_map/while
  310.3 14.3 %copy-start.3 = (pred[256,1024]{1,0:T(8,128)(4,1)}, pred[256,1024]{1,0:T(8,128)(4,1)S(1)}, u32[]{:S(2)}) copy-start(pred[256,1024]{1,0:T(8,128)(4,1)S(1)} %broadcast_compare_fusion.5) | copy-start | bytes 786436 | tf_op jit(solution)/shard_map/while
  313.0 11.6 %slice-start = ((s8[12582912]{0:T(1024)(128)(4,1)}), s8[4194304]{0:T(1024)(128)(4,1)S(1)}, s32[]{:S(2)}) async-start(s8[12582912]{0:T(1024)(128)(4,1)} %bitcast.175), calls=%async_computation.24 | async-start | bytes 8388608 | tf_op jit(solution)/shard_map/while
  313.0 11.6 %slice-start.1 = ((s8[12582912]{0:T(1024)(128)(4,1)}), s8[4194304]{0:T(1024)(128)(4,1)S(1)}, s32[]{:S(2)}) async-start(s8[12582912]{0:T(1024)(128)(4,1)} %bitcast.175), calls=%async_computation.25 | async-start | bytes 8388608 | tf_op jit(solution)/shard_map/while
  313.0 12.6 %slice-start.2 = ((s8[12582912]{0:T(1024)(128)(4,1)}), s8[4194304]{0:T(1024)(128)(4,1)S(1)}, s32[]{:S(2)}) async-start(s8[12582912]{0:T(1024)(128)(4,1)} %bitcast.175), calls=%async_computation.26 | async-start | bytes 8388608 | tf_op jit(solution)/shard_map/while
  348.2 4.4 copy-start.1
  355.4 78.6 %reduce-scatter.11.cloned.1.call-start = ((), (), s32[]{:S(2)}) async-start(), calls=%async_computation.17 | async-start | bytes 3932160 | tf_op jit(solution)/shard_map/reduce_scatter | solution.py:225
  356.0 109.3 %reduce-scatter.13.cloned.1.call-start = ((), (), s32[]{:S(2)}) async-start(), calls=%async_computation.18 | async-start | bytes 1474560 | tf_op jit(solution)/shard_map/reduce_scatter | solution.py:261
  358.3 3.1 copy-start.11
  361.4 130.0 %reduce-scatter.19.cloned.1.call-start = ((), (), s32[]{:S(2)}) async-start(), calls=%async_computation.21 | async-start | bytes 1474560 | tf_op jit(solution)/shard_map/reduce_scatter | solution.py:270
  364.4 156.7 %reduce-scatter.15.cloned.1.call-start = ((), (), s32[]{:S(2)}) async-start(), calls=%async_computation.19 | async-start | bytes 1474560 | tf_op jit(solution)/shard_map/reduce_scatter | solution.py:264
  396.8 40.6 %copy-start.43 = (f32[512]{0:T(512)S(1)}, f32[512]{0:T(512)}, u32[]{:S(2)}) copy-start(f32[512]{0:T(512)} %copy-done.42) | copy-start | bytes 6148
  396.8 40.6 %copy-start.47 = (f32[768]{0:T(1024)S(1)}, f32[768]{0:T(1024)}, u32[]{:S(2)}) copy-start(f32[768]{0:T(1024)} %copy-done.46) | copy-start | bytes 9220
  396.8 40.6 %copy-start.54 = (f32[512]{0:T(512)S(1)}, f32[512]{0:T(512)}, u32[]{:S(2)}) copy-start(f32[512]{0:T(512)} %copy-done.53) | copy-start | bytes 6148
  396.8 40.6 %copy-start.58 = (f32[768]{0:T(1024)S(1)}, f32[768]{0:T(1024)}, u32[]{:S(2)}) copy-start(f32[768]{0:T(1024)} %copy-done.57) | copy-start | bytes 9220
  396.8 151.8 %reduce-scatter.17.cloned.1.call-start = ((), (), s32[]{:S(2)}) async-start(), calls=%async_computation.20 | async-start | bytes 1474560 | tf_op jit(solution)/shard_map/reduce_scatter | solution.py:267
  437.4 161.5 %reduce-scatter.21.cloned.1.call-start = ((), (), s32[]{:S(2)}) async-start(), calls=%async_computation.22 | async-start | bytes 5898240 | tf_op jit(solution)/shard_map/reduce_scatter | solution.py:198
  444.9 204.4 %reduce-scatter.23.cloned.1.call-start = ((), (), s32[]{:S(2)}) async-start(), calls=%async_computation.23 | async-start | bytes 5898240 | tf_op jit(solution)/shard_map/reduce_scatter | solution.py:201
  508.6 3.2 copy-start.16
  511.8 137.5 %copy-start.28 = (bf16[768,192]{0,1:T(8,128)(2,1)S(1)}, bf16[768,192]{0,1:T(8,128)(2,1)}, u32[]{:S(2)}) copy-start(bf16[768,192]{0,1:T(8,128)(2,1)} %reduce-scatter.13.cloned.1.call-done) | copy-start | bytes 884740
  511.8 137.5 %copy-start.29 = (bf16[192,768]{1,0:T(8,128)(2,1)S(1)}, bf16[192,768]{1,0:T(8,128)(2,1)}, u32[]{:S(2)}) copy-start(bf16[192,768]{1,0:T(8,128)(2,1)} %reduce-scatter.19.cloned.1.call-done) | copy-start | bytes 884740
  (43 other events, 79.7 us)
Sparse Core Ops, SparseCore 0:
  10.3 20.2 all-gather.9
  32.7 17.4 all-gather.15
  52.3 17.5 all-gather.13
  71.9 28.9 all-gather.11
  102.2 28.9 all-gather.17
  133.2 17.4 all-gather.19
  152.8 37.4 all-gather.21
  192.5 37.4 all-gather.23
  355.6 37.9 reduce-scatter.8
  396.1 37.9 reduce-scatter.10
  437.2 25.7 reduce-scatter.12
  465.6 25.7 reduce-scatter.18
  494.5 25.7 reduce-scatter.14
  522.8 25.7 reduce-scatter.16
  551.0 47.8 reduce-scatter.20
  601.4 47.8 reduce-scatter.22
where the time goes:
time: 942 us; the launch traced here: 935 us
  waiting for transfers between devices  356 us (38%)
  blocking collectives  308 us (33%)
  matrix products  151 us (16%)
  local copies, waits for them, and re-layouts  54.9 us (6%)
  other arithmetic  47.5 us (5%)
  between operations  17 us (2%)
    psum x1, blocking collectives, per_device(): lax.psum((grad_query_full, grad_key_full, grad_value_full, grad_out_full,...  279 us
    reduce_scatter x1, waiting for transfers between devices, per_device(): lax.psum_scatter(grad_fc2.astype(jnp.bfloat16), 'group', scatter_dimensio...  50.5 us
    reduce_scatter x1, waiting for transfers between devices, per_device(): lax.psum_scatter(grad_fc1.astype(jnp.bfloat16), 'group', scatter_dimensio...  50.2 us
    reduce_scatter x1, waiting for transfers between devices, per_device(): lax.psum_scatter(value_parts.astype(jnp.bfloat16), 'group', scatter_dimen...  37.2 us
    all_gather x1, waiting for transfers between devices, per_device(): lax.all_gather(w_fc2.astype(jnp.bfloat16), 'group', axis=0, tiled=True)  31.4 us
    all_gather x1, waiting for transfers between devices, per_device(): lax.all_gather(keys_new.reshape(row_block, local_len, width), 'group', ax...  30.4 us
    reduce_scatter x1, waiting for transfers between devices, per_device(): lax.psum_scatter(key_parts.astype(jnp.bfloat16), 'group', scatter_dimensi...  29.1 us
    all_gather x1, waiting for transfers between devices, per_device(): lax.all_gather(values_new.reshape(row_block, local_len, width), 'group',...  28.4 us
  transfers between devices with their start and end apart: 16, of which 13 were waited for; matrix products, arithmetic and copies ran while one was open for 13% of the time, Pallas kernels for 0%

commit v1 on v0

--- a/solution.py
+++ b/solution.py
@@ -7,6 +7,27 @@
 HEAD_DIM = 64
 EPS = 1e-06
 MASKED = -1e30
+
+
+def ring_gather(array, axis, dim):
+    devices, position, rows = (lax.axis_size(axis), lax.axis_index(axis), array.shape[dim])
+    right = [(i, (i + 1) % devices) for i in range(devices)]
+    backward = [(i, (i - 1) % devices) for i in range(devices)]
+    out = jnp.zeros((*array.shape[:dim], devices * rows, *array.shape[dim + 1 :]), array.dtype)
+    out = lax.dynamic_update_slice_in_dim(out, array, position * rows, axis=dim)
+    from_left = from_right = array
+    half = devices // 2
+    for step in range(1, half + 1):
+        from_left = lax.ppermute(from_left, axis, right)
+        out = lax.dynamic_update_slice_in_dim(
+            out, from_left, (position - step) % devices * rows, axis=dim
+        )
+        if step < devices - half:
+            from_right = lax.ppermute(from_right, axis, backward)
+            out = lax.dynamic_update_slice_in_dim(
+                out, from_right, (position + step) % devices * rows, axis=dim
+            )
+    return out
 
 
 def to_float(values):
@@ -175,7 +196,7 @@
     hat_two, inverse_two = normalize(middle)
     normed_two = (hat_two * to_float(gain_two) + to_float(shift_two)).astype(jnp.bfloat16)
     fc1_full, fc2_full, bias_fc1 = (
-        lax.all_gather(w_fc1.astype(jnp.bfloat16), "group", axis=1, tiled=True),
+        ring_gather(w_fc1.astype(jnp.bfloat16), "group", 1),
         lax.all_gather(w_fc2.astype(jnp.bfloat16), "group", axis=0, tiled=True),
         lax.all_gather(fc1_bias.astype(jnp.bfloat16), "group", axis=0, tiled=True),
     )

time: 942 us -> 918 us (0.975)
  waiting for transfers between devices: 356 us -> 305 us
  blocking collectives: 308 us -> 331 us
    ppermute x0 -> x3, waiting for transfers between devices: none -> 31 us  [the longest x2 31 us: ring_gather(): from_left = lax.ppermute(from_left, axis, right)]
    all_gather x1, waiting for transfers between devices: 28.4 us -> 0.01 us  [per_device(): lax.all_gather(values_new.reshape(row_block, local_len, width), 'group',...]
    all_gather x1 -> x0, waiting for transfers between devices: 25.6 us -> none  [per_device(): lax.all_gather(w_fc1.astype(jnp.bfloat16), 'group', axis=1, tiled=True)]
    all_gather x1, blocking collectives: 5.2 us -> 28.7 us  [per_device(): lax.all_gather(fc1_bias.astype(jnp.bfloat16), 'group', axis=0, tiled=True)]
    all_gather x1, waiting for transfers between devices: 30.4 us -> 13.5 us  [per_device(): lax.all_gather(keys_new.reshape(row_block, local_len, width), 'group', ax...]
    all_gather x1, waiting for transfers between devices: 31.4 us -> 20.7 us  [per_device(): lax.all_gather(w_fc2.astype(jnp.bfloat16), 'group', axis=0, tiled=True)]
  transfers between devices with their start and end apart: 16 -> 18, of which waited for: 13 -> 11; matrix products, arithmetic and copies ran while one was open for 13% -> 14% of each run, Pallas kernels for 0% -> 0%
where the time goes in v1:
time: 918 us; the launch traced here: 911 us
  blocking collectives  331 us (36%)
  waiting for transfers between devices  305 us (33%)
  matrix products  147 us (16%)
  local copies, waits for them, and re-layouts  64.2 us (7%)
  other arithmetic  44.2 us (5%)
  between operations  17 us (2%)
    psum x1, blocking collectives, per_device(): lax.psum((grad_query_full, grad_key_full, grad_value_full, grad_out_full,...  279 us
    reduce_scatter x1, waiting for transfers between devices, per_device(): lax.psum_scatter(grad_fc1.astype(jnp.bfloat16), 'group', scatter_dimensio...  50.4 us
    reduce_scatter x1, waiting for transfers between devices, per_device(): lax.psum_scatter(grad_fc2.astype(jnp.bfloat16), 'group', scatter_dimensio...  50.3 us
    reduce_scatter x1, waiting for transfers between devices, per_device(): lax.psum_scatter(value_parts.astype(jnp.bfloat16), 'group', scatter_dimen...  37.4 us
    ppermute x2, waiting for transfers between devices, ring_gather(): from_left = lax.ppermute(from_left, axis, right)  31 us
    reduce_scatter x1, waiting for transfers between devices, per_device(): lax.psum_scatter(key_parts.astype(jnp.bfloat16), 'group', scatter_dimensi...  29.1 us
    all_gather x1, blocking collectives, per_device(): lax.all_gather(fc1_bias.astype(jnp.bfloat16), 'group', axis=0, tiled=True)  28.7 us
    reduce_scatter x1, waiting for transfers between devices, per_device(): lax.psum_scatter(grad_value_full.astype(jnp.bfloat16), 'group', scatter_d...  27.5 us
  transfers between devices with their start and end apart: 18, of which 11 were waited for; matrix products, arithmetic and copies ran while one was open for 14% of the time, Pallas kernels for 0%

profile of v1, /device:TPU:0, one launch (start us, length us, event | category | flops | bytes accessed | tf_op | source)
XLA Modules:
  0.0 910.6 jit_solution(6277222071585377412)
XLA Ops:
  7.3 1.9 convert_element_type.265
  13.8 13.2 %all-reduce.19 = (bf16[768]{0:T(1024)(128)(2,1)S(1)}, bf16[768]{0:T(1024)(128)(2,1)S(1)}, bf16[768]{0:T(1024)(128)(2,1)S(1)}, bf16[768]{0:T(1024)(128)(2,1)S(1)}...) all-reduce(bf16[768]{0:T(1024)(128)(2,1)S(1)} %dynamic-update-slice, ...), channel_id=1, replica_groups=mesh['group'=4,'replica'=8] {'group'}, use_global_device_ids=true, to_apply=%add.1 | all-reduce | flops 5376 | bytes 21504
  30.6 2.1 add_convert_fusion.3
  33.9 16.3 %all-gather.15.cloned.1.call-done = bf16[768,768]{0,1:T(8,128)(2,1)} async-done(((bf16[768,192]{0,1:T(8,128)(2,1)}), bf16[768,768]{0,1:T(8,128)(2,1)}) %all-gather.15.cloned.1.call-update) | async-done | bytes 1179664 | tf_op jit(solution)/shard_map/all_gather | solution.py:160
  50.2 2.1 convolution_convert_fusion.4
  57.6 1.9 copy-done.19
  61.6 31.0 %collective-permute-done = bf16[768,768]{1,0:T(8,128)(2,1)} collective-permute-done((bf16[768,768]{1,0:T(8,128)(2,1)}, bf16[768,768]{1,0:T(8,128)(2,1)}, u32[]{:S(2)}, u32[]{:S(2)}) %collective-permute-start) | collective-permute-done | bytes 1179680 | tf_op jit(solution)/shard_map/ppermute | solution.py:21
  93.8 28.7 %all-gather = bf16[4,1,768]{2,1,0:T(2,128)(2,1)S(1)} all-gather(bf16[1,1,768]{2,1,0:T(2,128)(2,1)S(1)} %reshape.383), channel_id=1, replica_groups=mesh['group'=4,'replica'=8] {'group'}, dimensions={0}, use_global_device_ids=true | all-gather | bytes 7680 | tf_op jit(solution)/shard_map/all_gather | solution.py:201
  124.2 2.6 constant_dynamic-update-slice_fusion.6
  126.8 2.6 constant_dynamic-update-slice_fusion.5
  129.4 2.1 add_convert_fusion.2
  131.8 2.4 constant_dynamic-update-slice_fusion.4
  134.2 13.5 %all-gather.17.cloned.1.call-done = bf16[2,1024,768]{1,2,0:T(8,128)(2,1)} async-done(((bf16[2,256,768]{1,2,0:T(8,128)(2,1)}), bf16[2,1024,768]{1,2,0:T(8,128)(2,1)}) %all-gather.17.cloned.1.call-update) | async-done | bytes 3145744 | tf_op jit(solution)/shard_map/all_gather | solution.py:185
  147.6 29.5 %while.26 = (s32[]{:T(128)}, bf16[2,256,768]{2,1,0:T(8,128)(2,1)}, f32[2,12,256]{2,1,0:T(8,128)}, bf16[2,1024,768]{1,2,0:T(8,128)(2,1)}, s32[2,256]{1,0:T(2,128)...) while((s32[]{:T(128)}, bf16[2,256,768]{2,1,0:T(8,128)(2,1)}, ...), condition=%wide.region_5.6_spmd, body=%wide.region_2.5_spmd.sunk | while | flops 843510784 | bytes 51499116 | solution.py:191
  148.7 2.2 constant_dynamic-slice_fusion.23
  151.0 2.3 fusion.100
  153.3 3.6 fusion.101
  157.6 3.9 fusion.102
  163.4 2.2 constant_dynamic-slice_fusion.23
  165.7 2.3 fusion.100
  168.0 3.6 fusion.101
  172.2 3.9 fusion.102
  177.1 2.8 fusion.32
  181.1 4.9 fusion.28
  186.1 20.7 %all-gather.21.cloned.1.call-done = bf16[3072,768]{1,0:T(8,128)(2,1)} async-done(((bf16[768,768]{1,0:T(8,128)(2,1)}), bf16[3072,768]{1,0:T(8,128)(2,1)}) %all-gather.21.cloned.1.call-update) | async-done | bytes 4718608 | tf_op jit(solution)/shard_map/all_gather | solution.py:200
  206.8 9.7 %fusion.29 = (bf16[3072]{0:T(1024)(128)(2,1)}, bf16[512,3072]{1,0:T(8,128)(2,1)S(1)}) fusion(f32[512,3072]{1,0:T(8,128)} %fusion.28, f32[3072]{0:T(1024)S(1)} %bitcast.214, bf16[512,768]{1,0:T(8,128)(2,1)S(1)} %copy-done.26, bf16[3072,768]{1,0:T(8,128)(2,1)} %all-gather.21.cloned.1.call-done), kind=kOutput, calls=%fused_computation.112 | convolution fusion | flops 2450519040 | bytes 14960640 | tf_op jit(solution)/shard_map/dot_general | solution.py:212
  216.6 3.5 multiply_reduce_fusion.1
  222.5 108.3 %while.27 = (s32[]{:T(128)}, bf16[2,256,768]{1,2,0:T(8,128)(2,1)}, bf16[2,1024,768]{2,1,0:T(8,128)(2,1)}, bf16[2,1024,768]{2,1,0:T(8,128)(2,1)}, bf16[2,1024,768...) while((s32[]{:T(128)}, bf16[2,256,768]{1,2,0:T(8,128)(2,1)}, ...), condition=%wide.region_12.13_spmd, body=%wide.region_10.12_spmd.sunk | while | flops 2062676992 | bytes 238113392 | solution.py:239
  223.0 2.1 constant_dynamic-slice_fusion.27
  225.1 6.4 fusion.113
  234.5 11.5 %multiply_reduce_fusion.10 = (f32[12,256]{1,0:T(8,128)S(1)}, f32[12,256,1024]{2,1,0:T(8,128)}) fusion(f32[12,256,1024]{2,1,0:T(8,128)} %fusion.113, f32[12,256]{1,0:T(8,128)S(1)} %dynamic-slice_bitcast_fusion.2, pred[256,1024]{1,0:T(8,128)(4,1)S(1)} %broadcast_compare_fusion.5, bf16[256,12,64]{0,2,1:T(8,128)(2,1)S(1)} %bitcast.188, ...), kind=kOutput, calls=%fused_computation.18.clone.1 | convolution fusion | flops 418378752 | bytes 27418624 | tf_op jit(solution)/shard_map/while/body/eval_jaxpr/qhe,khe->hqk/dot_general | solution.py:94
  247.1 6.7 multiply_convert_fusion.6
  257.9 9.0 fusion.115
  267.0 2.7 copy.97
  269.7 3.4 constant_dynamic-update-slice_fusion.13
  274.1 2.0 fusion.114
  276.9 2.1 constant_dynamic-slice_fusion.27
  279.1 6.4 fusion.113
  288.4 11.5 %multiply_reduce_fusion.10 = (f32[12,256]{1,0:T(8,128)S(1)}, f32[12,256,1024]{2,1,0:T(8,128)}) fusion(f32[12,256,1024]{2,1,0:T(8,128)} %fusion.113, f32[12,256]{1,0:T(8,128)S(1)} %dynamic-slice_bitcast_fusion.2, pred[256,1024]{1,0:T(8,128)(4,1)S(1)} %broadcast_compare_fusion.5, bf16[256,12,64]{0,2,1:T(8,128)(2,1)S(1)} %bitcast.188, ...), kind=kOutput, calls=%fused_computation.18.clone.1 | convolution fusion | flops 418378752 | bytes 27418624 | tf_op jit(solution)/shard_map/while/body/eval_jaxpr/qhe,khe->hqk/dot_general | solution.py:94
  301.0 6.7 multiply_convert_fusion.6
  311.9 9.0 fusion.115
  320.9 2.7 copy.97
  323.6 3.4 constant_dynamic-update-slice_fusion.13
  328.0 2.0 fusion.114
  333.7 3.0 bitcast_convert_fusion.2
  336.9 3.0 convolution_convert_fusion.2
  339.9 29.1 %reduce-scatter.9.cloned.1.call-done = bf16[2,256,768]{2,1,0:T(8,128)(2,1)} async-done(((bf16[2,1024,768]{2,1,0:T(8,128)(2,1)}), bf16[2,256,768]{2,1,0:T(8,128)(2,1)}) %reduce-scatter.9.cloned.1.call-update) | async-done | bytes 786448 | tf_op jit(solution)/shard_map/reduce_scatter | solution.py:243
  369.0 3.2 bitcast_convert_fusion.1
  372.3 37.4 %reduce-scatter.11.cloned.1.call-done = bf16[2,256,768]{2,1,0:T(8,128)(2,1)} async-done(((bf16[2,1024,768]{2,1,0:T(8,128)(2,1)}), bf16[2,256,768]{2,1,0:T(8,128)(2,1)}) %reduce-scatter.11.cloned.1.call-update) | async-done | bytes 786448 | tf_op jit(solution)/shard_map/reduce_scatter | solution.py:246
  409.7 3.2 bitcast_convert_fusion
  413.0 8.9 convolution_convert_fusion
  422.5 7.4 convolution_convert_fusion.1
  433.8 2.3 copy.57
  437.4 3.5 fusion.34
  440.9 26.1 %reduce-scatter.19.cloned.1.call-done = bf16[192,768]{1,0:T(8,128)(2,1)} async-done(((bf16[768,768]{1,0:T(8,128)(2,1)}), bf16[192,768]{1,0:T(8,128)(2,1)}) %reduce-scatter.19.cloned.1.call-update) | async-done | bytes 294928 | tf_op jit(solution)/shard_map/reduce_scatter | solution.py:291
  468.3 2.4 fusion.35
  470.8 2.4 multiply_reduce_fusion.2
  473.3 10.3 %all-reduce.18 = (bf16[768]{0:T(1024)(128)(2,1)S(1)}, bf16[768]{0:T(1024)(128)(2,1)S(1)}, bf16[768]{0:T(1024)(128)(2,1)S(1)}, bf16[768]{0:T(1024)(128)(2,1)S(1)}...) all-reduce(bf16[768]{0:T(1024)(128)(2,1)S(1)} %dynamic-update-slice, ...), channel_id=1, replica_groups=mesh['group'=4,'replica'=8] {'group'}, use_global_device_ids=true, to_apply=%add.7 | all-reduce | flops 9984 | bytes 39936
  484.2 3.2 multiply_add_fusion
  487.4 9.3 %add_add_fusion.1 = f32[512,768]{1,0:T(8,128)} fusion(f32[512,768]{1,0:T(8,128)S(1)} %copy-done.16, bf16[3072,768]{1,0:T(8,128)(2,1)} %all-gather.21.cloned.1.call-done, f32[768]{0:T(1024)S(1)} %convert_element_type.289, f32[512,3072]{1,0:T(8,128)} %fusion.28, f32[3072]{0:T(1024)S(1)} %bitcast.216), kind=kOutput, calls=%fused_computation.67 | convolution fusion | flops 2432434176 | bytes 14171136 | tf_op jit(solution)/shard_map/dot_general | solution.py:206
  496.7 27.5 %reduce-scatter.17.cloned.1.call-done = bf16[768,192]{0,1:T(8,128)(2,1)} async-done(((bf16[768,768]{0,1:T(8,128)(2,1)}), bf16[768,192]{0,1:T(8,128)(2,1)}) %reduce-scatter.17.cloned.1.call-update) | async-done | bytes 294928 | tf_op jit(solution)/shard_map/reduce_scatter | solution.py:288
  524.2 50.3 %reduce-scatter.23.cloned.1.call-done = bf16[768,768]{1,0:T(8,128)(2,1)} async-done(((bf16[3072,768]{1,0:T(8,128)(2,1)}), bf16[768,768]{1,0:T(8,128)(2,1)}) %reduce-scatter.23.cloned.1.call-update) | async-done | bytes 1179664 | tf_op jit(solution)/shard_map/reduce_scatter | solution.py:222
  574.4 50.4 %reduce-scatter.21.cloned.1.call-done = bf16[768,768]{1,0:T(8,128)(2,1)} async-done(((bf16[768,3072]{1,0:T(8,128)(2,1)}), bf16[768,768]{1,0:T(8,128)(2,1)}) %reduce-scatter.21.cloned.1.call-update) | async-done | bytes 1179664 | tf_op jit(solution)/shard_map/reduce_scatter | solution.py:219
  624.9 279.0 %all-reduce.21 = (f32[192]{0:T(256)}, f32[192]{0:T(256)}, f32[768,192]{0,1:T(8,128)}, f32[192]{0:T(256)}, f32[768,192]{0,1:T(8,128)}, /*index=5*/f32[768,192]{0,...) all-reduce(f32[192]{0:T(256)S(1)} %dynamic-slice_convert_fusion.8, ...), channel_id=1, replica_groups=mesh['group'=4,'replica'=8] {'replica'}, use_global_device_ids=true, to_apply=%region_19.20 | all-reduce | flops 1771776 | bytes 10635264 | tf_op jit(solution)/shard_map/psum | solution.py:335
  (361 shorter events, 56.8 us)
Async XLA Ops:
  7.2 3.7 copy-start.70
  7.2 3.8 copy-start.71
  7.2 3.8 copy-start.72
  7.2 3.8 copy-start.73
  7.3 3.8 copy-start.74
  7.3 3.8 copy-start.75
  7.3 3.8 copy-start.76
  7.3 23.3 %all-gather.9.cloned.1.call-start = ((), (), s32[]{:S(2)}) async-start(), calls=%async_computation.8 | async-start | bytes 1474560 | tf_op jit(solution)/shard_map/all_gather | solution.py:161
  9.2 17.8 %copy-start.5 = (f32[2,256,768]{2,1,0:T(8,128)S(1)}, f32[2,256,768]{2,1,0:T(8,128)}, u32[]{:S(2)}) copy-start(f32[2,256,768]{2,1,0:T(8,128)} %param.22) | copy-start | bytes 4718596
  9.2 41.0 %all-gather.15.cloned.1.call-start = ((), (), s32[]{:S(2)}) async-start(), calls=%async_computation.11 | async-start | bytes 1474560 | tf_op jit(solution)/shard_map/all_gather | solution.py:160
  10.1 119.3 %all-gather.13.cloned.1.call-start = ((), (), s32[]{:S(2)}) async-start(), calls=%async_computation.10 | async-start | bytes 1474560 | tf_op jit(solution)/shard_map/all_gather | solution.py:159
  10.9 123.3 %all-gather.11.cloned.1.call-start = ((), (), s32[]{:S(2)}) async-start(), calls=%async_computation.9 | async-start | bytes 3932160 | tf_op jit(solution)/shard_map/all_gather | solution.py:186
  28.7 21.5 %copy-start.27 = (bf16[512,768]{1,0:T(8,128)(2,1)}, bf16[512,768]{1,0:T(8,128)(2,1)S(1)}, u32[]{:S(2)}) copy-start(bf16[512,768]{1,0:T(8,128)(2,1)S(1)} %add_convert_fusion.4) | copy-start | bytes 2359300
  33.8 113.8 %all-gather.17.cloned.1.call-start = ((), (), s32[]{:S(2)}) async-start(), calls=%async_computation.12 | async-start | bytes 3932160 | tf_op jit(solution)/shard_map/all_gather | solution.py:185
  53.5 123.6 %all-gather.19.cloned.1.call-start = ((), (), s32[]{:S(2)}) async-start(), calls=%async_computation.13 | async-start | bytes 1474560 | tf_op jit(solution)/shard_map/all_gather | solution.py:162
  54.3 152.5 %all-gather.21.cloned.1.call-start = ((), (), s32[]{:S(2)}) async-start(), calls=%async_computation.14 | async-start | bytes 5898240 | tf_op jit(solution)/shard_map/all_gather | solution.py:200
  56.1 3.6 copy-start.23
  57.3 36.5 %copy-start.62 = (f32[768]{0:T(1024)S(1)}, f32[768]{0:T(1024)}, u32[]{:S(2)}) copy-start(f32[768]{0:T(1024)} %param.37) | copy-start | bytes 9220
  57.3 35.2 %collective-permute-start = (bf16[768,768]{1,0:T(8,128)(2,1)}, bf16[768,768]{1,0:T(8,128)(2,1)}, u32[]{:S(2)}, u32[]{:S(2)}) collective-permute-start(bf16[768,768]{1,0:T(8,128)(2,1)} %get-tuple-element.266), channel_id=1, source_target_pairs={{0,8},{8,16},{16,24},{24,0},{1,9},{9,17},{17,25},{25,1},{2,10},{10... | collective-permute-start | bytes 3538952 | tf_op jit(solution)/shard_map/ppermute | solution.py:21
  59.5 67.3 %collective-permute-start.1 = (bf16[768,768]{1,0:T(8,128)(2,1)}, bf16[768,768]{1,0:T(8,128)(2,1)}, u32[]{:S(2)}, u32[]{:S(2)}) collective-permute-start(bf16[768,768]{1,0:T(8,128)(2,1)} %get-tuple-element.266), channel_id=1, source_target_pairs={{0,24},{8,0},{16,8},{24,16},{1,25},{9,1},{17,9},{25,17},{2,26},{10... | collective-permute-start | bytes 3538952 | tf_op jit(solution)/shard_map/ppermute | solution.py:26
  59.7 63.5 %copy-start.12 = (f32[2,256,768]{2,1,0:T(8,128)S(1)}, f32[2,256,768]{2,1,0:T(8,128)}, u32[]{:S(2)}) copy-start(f32[2,256,768]{2,1,0:T(8,128)} %param.23) | copy-start | bytes 4718596
  60.8 308.2 %reduce-scatter.9.cloned.1.call-start = ((), (), s32[]{:S(2)}) async-start(), calls=%async_computation.15 | async-start | bytes 3932160 | tf_op jit(solution)/shard_map/reduce_scatter | solution.py:243
  61.6 158.6 %copy-start.52 = (f32[768]{0:T(1024)}, f32[768]{0:T(1024)S(1)}, u32[]{:S(2)}) copy-start(f32[768]{0:T(1024)S(1)} %convert_element_type.279) | copy-start | bytes 9220
  61.6 118.7 %copy-start.63 = (f32[768]{0:T(1024)}, f32[768]{0:T(1024)S(1)}, u32[]{:S(2)}) copy-start(f32[768]{0:T(1024)S(1)} %convert_element_type.281) | copy-start | bytes 9220
  92.5 39.2 %collective-permute-start.2 = (bf16[768,768]{1,0:T(8,128)(2,1)}, bf16[768,768]{1,0:T(8,128)(2,1)}, u32[]{:S(2)}, u32[]{:S(2)}) collective-permute-start(bf16[768,768]{1,0:T(8,128)(2,1)} %collective-permute-done), channel_id=1, source_target_pairs={{0,8},{8,16},{16,24},{24,0},{1,9},{9,17},{17,25},{25,1},{2,10},{10... | collective-permute-start | bytes 3538952 | tf_op jit(solution)/shard_map/ppermute | solution.py:21
  93.8 33.0 %copy-start.50 = (f32[1,2,2,128]{3,1,2,0:T(2,128)}, f32[1,2,2,128]{3,1,2,0:T(2,128)S(1)}, u32[]{:S(2)}) copy-start(f32[1,2,2,128]{3,1,2,0:T(2,128)S(1)} %copy.90) | copy-start | bytes 6148
  177.1 4.0 copy-start.20
  180.0 40.1 %copy-start.48 = (f32[512]{0:T(512)}, f32[512]{0:T(512)S(1)}, u32[]{:S(2)}) copy-start(f32[512]{0:T(512)S(1)} %broadcast_multiply_fusion.4) | copy-start | bytes 6148
  181.1 39.0 %copy-start.59 = (f32[512]{0:T(512)}, f32[512]{0:T(512)S(1)}, u32[]{:S(2)}) copy-start(f32[512]{0:T(512)S(1)} %add_rsqrt_fusion) | copy-start | bytes 6148
  181.1 25.7 %copy-start.26 = (bf16[512,768]{1,0:T(8,128)(2,1)S(1)}, bf16[512,768]{1,0:T(8,128)(2,1)}, u32[]{:S(2)}) copy-start(bf16[512,768]{1,0:T(8,128)(2,1)} %fusion.21) | copy-start | bytes 2359300
  181.1 25.7 %copy-start.54 = (f32[4,1,768]{2,1,0:T(1,128)S(1)}, f32[4,1,768]{2,1,0:T(1,128)}, u32[]{:S(2)}) copy-start(f32[4,1,768]{2,1,0:T(1,128)} %convert_element_type.326) | copy-start | bytes 36868
  181.1 35.4 %slice-start.3 = ((s8[4718592]{0:T(1024)(128)(4,1)}), s8[524288]{0:T(1024)(128)(4,1)S(1)}, s32[]{:S(2)}) async-start(s8[4718592]{0:T(1024)(128)(4,1)} %bitcast.192), calls=%async_computation.26 | async-start | bytes 1048576
  206.8 9.7 %copy-start.15 = (f32[512,768]{1,0:T(8,128)S(1)}, f32[512,768]{1,0:T(8,128)}, u32[]{:S(2)}) copy-start(f32[512,768]{1,0:T(8,128)} %copy-done.14) | copy-start | bytes 4718596
  206.8 9.7 %slice-start.4 = ((s8[4718592]{0:T(1024)(128)(4,1)}), s8[4194304]{0:T(1024)(128)(4,1)S(1)}, s32[]{:S(2)}) async-start(s8[4718592]{0:T(1024)(128)(4,1)} %bitcast.192), calls=%async_computation.27 | async-start | bytes 8388608
  216.5 3.6 copy-start.78
  216.6 3.6 copy-start.13
  216.6 3.6 copy-start.51
  222.9 9.3 %copy-start.38 = (s32[2,256]{1,0:T(2,128)}, s32[2,256]{1,0:T(2,128)S(1)}, u32[]{:S(2)}) copy-start(s32[2,256]{1,0:T(2,128)S(1)} %get-tuple-element.475) | copy-start | bytes 6148 | tf_op jit(solution)/shard_map/while
  223.0 9.5 %copy-start.17 = (bf16[2,256,768]{2,1,0:T(8,128)(2,1)}, bf16[2,256,768]{2,1,0:T(8,128)(2,1)S(1)}, u32[]{:S(2)}) copy-start(bf16[2,256,768]{2,1,0:T(8,128)(2,1)S(1)} %get-tuple-element.479) | copy-start | bytes 2359300 | tf_op jit(solution)/shard_map/while
  225.1 7.4 copy-start.35
  232.5 13.5 %copy-start.3 = (pred[256,1024]{1,0:T(8,128)(4,1)}, pred[256,1024]{1,0:T(8,128)(4,1)S(1)}, u32[]{:S(2)}) copy-start(pred[256,1024]{1,0:T(8,128)(4,1)S(1)} %broadcast_compare_fusion.5) | copy-start | bytes 786436 | tf_op jit(solution)/shard_map/while
  234.4 11.6 %slice-start = ((s8[12582912]{0:T(1024)(128)(4,1)}), s8[4194304]{0:T(1024)(128)(4,1)S(1)}, s32[]{:S(2)}) async-start(s8[12582912]{0:T(1024)(128)(4,1)} %bitcast.175), calls=%async_computation.23 | async-start | bytes 8388608 | tf_op jit(solution)/shard_map/while
  234.4 11.6 %slice-start.1 = ((s8[12582912]{0:T(1024)(128)(4,1)}), s8[4194304]{0:T(1024)(128)(4,1)S(1)}, s32[]{:S(2)}) async-start(s8[12582912]{0:T(1024)(128)(4,1)} %bitcast.175), calls=%async_computation.24 | async-start | bytes 8388608 | tf_op jit(solution)/shard_map/while
  234.4 12.6 %slice-start.2 = ((s8[12582912]{0:T(1024)(128)(4,1)}), s8[4194304]{0:T(1024)(128)(4,1)S(1)}, s32[]{:S(2)}) async-start(s8[12582912]{0:T(1024)(128)(4,1)} %bitcast.175), calls=%async_computation.25 | async-start | bytes 8388608 | tf_op jit(solution)/shard_map/while
  269.7 4.4 copy-start.1
  276.9 9.3 %copy-start.38 = (s32[2,256]{1,0:T(2,128)}, s32[2,256]{1,0:T(2,128)S(1)}, u32[]{:S(2)}) copy-start(s32[2,256]{1,0:T(2,128)S(1)} %get-tuple-element.475) | copy-start | bytes 6148 | tf_op jit(solution)/shard_map/while
  276.9 9.6 %copy-start.17 = (bf16[2,256,768]{2,1,0:T(8,128)(2,1)}, bf16[2,256,768]{2,1,0:T(8,128)(2,1)S(1)}, u32[]{:S(2)}) copy-start(bf16[2,256,768]{2,1,0:T(8,128)(2,1)S(1)} %get-tuple-element.479) | copy-start | bytes 2359300 | tf_op jit(solution)/shard_map/while
  279.1 7.4 copy-start.35
  286.4 13.5 %copy-start.3 = (pred[256,1024]{1,0:T(8,128)(4,1)}, pred[256,1024]{1,0:T(8,128)(4,1)S(1)}, u32[]{:S(2)}) copy-start(pred[256,1024]{1,0:T(8,128)(4,1)S(1)} %broadcast_compare_fusion.5) | copy-start | bytes 786436 | tf_op jit(solution)/shard_map/while
  288.4 11.6 %slice-start = ((s8[12582912]{0:T(1024)(128)(4,1)}), s8[4194304]{0:T(1024)(128)(4,1)S(1)}, s32[]{:S(2)}) async-start(s8[12582912]{0:T(1024)(128)(4,1)} %bitcast.175), calls=%async_computation.23 | async-start | bytes 8388608 | tf_op jit(solution)/shard_map/while
  288.4 11.6 %slice-start.1 = ((s8[12582912]{0:T(1024)(128)(4,1)}), s8[4194304]{0:T(1024)(128)(4,1)S(1)}, s32[]{:S(2)}) async-start(s8[12582912]{0:T(1024)(128)(4,1)} %bitcast.175), calls=%async_computation.24 | async-start | bytes 8388608 | tf_op jit(solution)/shard_map/while
  288.4 12.6 %slice-start.2 = ((s8[12582912]{0:T(1024)(128)(4,1)}), s8[4194304]{0:T(1024)(128)(4,1)S(1)}, s32[]{:S(2)}) async-start(s8[12582912]{0:T(1024)(128)(4,1)} %bitcast.175), calls=%async_computation.25 | async-start | bytes 8388608 | tf_op jit(solution)/shard_map/while
  323.6 4.4 copy-start.1
  330.9 78.8 %reduce-scatter.11.cloned.1.call-start = ((), (), s32[]{:S(2)}) async-start(), calls=%async_computation.16 | async-start | bytes 3932160 | tf_op jit(solution)/shard_map/reduce_scatter | solution.py:246
  331.6 109.3 %reduce-scatter.13.cloned.1.call-start = ((), (), s32[]{:S(2)}) async-start(), calls=%async_computation.17 | async-start | bytes 1474560 | tf_op jit(solution)/shard_map/reduce_scatter | solution.py:282
  336.8 130.1 %reduce-scatter.19.cloned.1.call-start = ((), (), s32[]{:S(2)}) async-start(), calls=%async_computation.20 | async-start | bytes 1474560 | tf_op jit(solution)/shard_map/reduce_scatter | solution.py:291
  339.9 156.8 %reduce-scatter.15.cloned.1.call-start = ((), (), s32[]{:S(2)}) async-start(), calls=%async_computation.18 | async-start | bytes 1474560 | tf_op jit(solution)/shard_map/reduce_scatter | solution.py:285
  372.2 40.7 %copy-start.55 = (f32[4,1,768]{2,1,0:T(1,128)S(1)}, f32[4,1,768]{2,1,0:T(1,128)}, u32[]{:S(2)}) copy-start(f32[4,1,768]{2,1,0:T(1,128)} %convert_element_type.326) | copy-start | bytes 36868
  372.2 151.9 %reduce-scatter.17.cloned.1.call-start = ((), (), s32[]{:S(2)}) async-start(), calls=%async_computation.19 | async-start | bytes 1474560 | tf_op jit(solution)/shard_map/reduce_scatter | solution.py:288
  412.9 161.5 %reduce-scatter.23.cloned.1.call-start = ((), (), s32[]{:S(2)}) async-start(), calls=%async_computation.22 | async-start | bytes 5898240 | tf_op jit(solution)/shard_map/reduce_scatter | solution.py:222
  421.9 203.0 %reduce-scatter.21.cloned.1.call-start = ((), (), s32[]{:S(2)}) async-start(), calls=%async_computation.21 | async-start | bytes 5898240 | tf_op jit(solution)/shard_map/reduce_scatter | solution.py:219
  484.2 3.2 copy-start.16
  487.4 137.5 %copy-start.33 = (bf16[768,192]{0,1:T(8,128)(2,1)S(1)}, bf16[768,192]{0,1:T(8,128)(2,1)}, u32[]{:S(2)}) copy-start(bf16[768,192]{0,1:T(8,128)(2,1)} %reduce-scatter.13.cloned.1.call-done) | copy-start | bytes 884740
  487.4 137.5 %copy-start.34 = (bf16[192,768]{1,0:T(8,128)(2,1)S(1)}, bf16[192,768]{1,0:T(8,128)(2,1)}, u32[]{:S(2)}) copy-start(bf16[192,768]{1,0:T(8,128)(2,1)} %reduce-scatter.19.cloned.1.call-done) | copy-start | bytes 884740
  (54 other events, 102.5 us)
Sparse Core Ops, SparseCore 0:
  10.3 20.2 all-gather.8
  32.7 17.4 all-gather.14
  52.3 23.6 all-gather.12
  78.0 39.2 all-gather.10
  118.7 28.9 all-gather.16
  149.6 17.4 all-gather.18
  169.3 37.4 all-gather.20
  331.0 37.9 reduce-scatter.8
  371.7 37.9 reduce-scatter.10
  412.7 25.7 reduce-scatter.12
  441.2 25.7 reduce-scatter.18
  469.9 25.7 reduce-scatter.14
  498.4 25.7 reduce-scatter.16
  526.6 47.8 reduce-scatter.22
  577.0 47.8 reduce-scatter.20
